TPU v7x, 32 devices: a whole 2x2x4 slice. The times are simulated.
32 devices in a mesh: chan: 8 (over z, y), seg: 4 (over x, core).
Axes of the slice: x: 2, y: 2, z: 4, core: 2. Of those that a mesh axis runs over, the one named last changes fastest.
Arguments:
- traces: bfloat16 [1024, 8192], P('chan', 'seg'), may hold values from -36 to 36
- pair_bins: int32 [2, 1024, 128], P(None, 'chan'), may hold values from 0 to 255
Outputs:
- correlograms: float32 [65, 256], P(None, 'chan')
All inputs are finite; a program needn't handle non-finite values.
Results may differ from a plain program's by a relative error of at most 0.0029.
Values may be sent and summed in bfloat16 or wider, within the bound.
A program may use at most 64 MiB of HBM per device.

v0:
```python
import math

import jax
import jax.numpy as jnp
from jax import lax
from jax.sharding import PartitionSpec as P

MAX_LAG = 32
NB = 256
ROUNDS = 2


EPSILON = 1e-06
LAG_GROUP = 13


def from_behind(block, axis, distance):
    devices = range(lax.axis_size(axis))
    route = [((i - distance) % len(devices), i) for i in devices]
    return lax.ppermute(block, axis, route)


def round_stack(own_block, own_scale, partner, partner_scale, round_bins, time_scale):
    channels, seg_length = own_block.shape
    lag_count = 2 * MAX_LAG + 1
    padded = jnp.pad(partner, ((0, 0), (MAX_LAG, MAX_LAG)))

    def lag_block(carry, group_index):
        window = lax.dynamic_slice_in_dim(
            padded, group_index * LAG_GROUP, seg_length + LAG_GROUP - 1, 1
        )
        pieces = []
        for offset in range(LAG_GROUP):
            shifted = window[:, offset : offset + seg_length]
            pieces.append(
                lax.dot_general(
                    own_block, shifted, (((1,), (1,)), ((), ())), preferred_element_type=jnp.float32
                )
            )
        return (carry, jnp.stack(pieces, 0))

    _, grouped = lax.scan(lag_block, 0, jnp.arange(lag_count // LAG_GROUP, dtype=jnp.int32))
    raw_sums = grouped.reshape(lag_count, channels, channels)
    zscore = raw_sums * own_scale[None, :, None] * partner_scale[None, None, :] * time_scale
    flat_scores = zscore.astype(jnp.bfloat16).reshape(lag_count, channels * channels)
    row_block = min(16, channels)
    width = row_block * channels
    bin_ids = jnp.arange(NB, dtype=jnp.int32)
    flat_bins = round_bins.reshape(channels * channels)

    def bin_step(running, block_index):
        score_piece = lax.dynamic_slice_in_dim(flat_scores, block_index * width, width, 1)
        bin_piece = lax.dynamic_slice_in_dim(flat_bins, block_index * width, width, 0)
        onehot = (bin_piece[:, None] == bin_ids[None, :]).astype(jnp.bfloat16)
        return (running + jnp.dot(score_piece, onehot, preferred_element_type=jnp.float32), None)

    running = jnp.zeros((lag_count, NB), jnp.float32)
    running, _ = lax.scan(bin_step, running, jnp.arange(channels // row_block, dtype=jnp.int32))
    return running


def squares(block):
    return jnp.sum(jnp.square(block.astype(jnp.float32)), axis=1)


def local(traces, pair_bins):
    channels, seg_length = traces.shape
    chan_count = lax.axis_size("chan")
    seg_count = lax.axis_size("seg")
    total_time = seg_length * seg_count
    time_scale = 1.0 / math.sqrt(total_time)
    half_loop = chan_count // 2
    far_block = from_behind(traces, "chan", -half_loop)
    near_block = from_behind(traces, "chan", 1 - half_loop)
    stacked = jnp.stack([squares(traces), squares(far_block), squares(near_block)], 0)
    energies = lax.psum(stacked, "seg")
    scales = lax.rsqrt(energies / total_time + EPSILON)
    partial_value = round_stack(traces, scales[0], far_block, scales[1], pair_bins[0], time_scale)
    partial_value = partial_value + round_stack(
        traces, scales[0], near_block, scales[2], pair_bins[1], time_scale
    )
    summed = lax.psum(partial_value, "seg")
    owned = lax.psum_scatter(summed, "chan", scatter_dimension=1, tiled=True)
    pair_total = ROUNDS * chan_count * channels * channels // NB
    return owned * (1.0 / math.sqrt(pair_total))


def solution(mesh):
    in_specs = (P("chan", "seg"), P(None, "chan", None))
    out_specs = P(None, "chan")
    return jax.shard_map(local, mesh=mesh, in_specs=in_specs, out_specs=out_specs, check_vma=False)
```

profile of v0, /device:TPU:0, one launch (start us, length us, event | category | flops | bytes accessed | tf_op | source)
XLA Modules:
  0.0 281.8 jit_solution(3189325173709044430)
XLA Ops:
  6.5 4.1 %collective-permute-start = (bf16[128,2048]{1,0:T(8,128)(2,1)}, bf16[128,2048]{1,0:T(8,128)(2,1)S(1)}, u32[]{:S(2)}, u32[]{:S(2)}) collective-permute-start(bf16[128,2048]{1,0:T(8,128)(2,1)} %param.10), channel_id=1, source_target_pairs={{16,0},{20,4},{24,8},{28,12},{0,16},{4,20},{8,24},{12,28},{17,1},{... | collective-permute-start | bytes 1572872 | tf_op jit(solution)/shard_map/ppermute | solution.py:20
  10.6 1.3 collective-permute-start.1
  11.9 1.3 multiply_reduce_fusion.2
  13.2 0.9 slice_bitcast_fusion
  14.1 32.1 %collective-permute-done = bf16[128,2048]{1,0:T(8,128)(2,1)S(1)} collective-permute-done((bf16[128,2048]{1,0:T(8,128)(2,1)}, bf16[128,2048]{1,0:T(8,128)(2,1)S(1)}, u32[]{:S(2)}, u32[]{:S(2)}) %collective-permute-start) | collective-permute-done | bytes 524320 | tf_op jit(solution)/shard_map/ppermute | solution.py:20
  46.5 5.7 %psum.14 = f32[3,128]{1,0:T(4,128)S(1)} all-reduce(f32[3,128]{1,0:T(4,128)S(1)} %pad_maximum_fusion), channel_id=1, replica_groups=mesh['chan'=8,'seg'=4] {'seg'}, use_global_device_ids=true, to_apply=%region_5.6 | all-reduce | flops 384 | bytes 3072 | tf_op jit(solution)/shard_map/psum | solution.py:76
  52.5 2.5 broadcast.29.clone2.1
  55.0 38.1 %while.42 = (s32[]{:T(128)}, f32[5,13,128,128]{3,2,1,0:T(8,128)}, s32[5]{0:T(128)S(1)}, bf16[128,2112]{1,0:T(8,128)(2,1)S(1)}, bf16[128,2048]{1,0:T(8,128)(2,1)S...) while((s32[]{:T(128)}, f32[5,13,128,128]{3,2,1,0:T(8,128)}, ...), condition=%wide.region_1.0_spmd, body=%wide.region_0.0_spmd.sunk | while | flops 872415232 | bytes 17892284 | solution.py:42
  61.6 1.0 constant_dynamic-update-slice_fusion.4
  69.2 1.0 constant_dynamic-update-slice_fusion.4
  76.9 1.0 constant_dynamic-update-slice_fusion.4
  84.5 1.0 constant_dynamic-update-slice_fusion.4
  92.1 1.0 constant_dynamic-update-slice_fusion.4
  93.1 2.9 %pad.12 = f32[72,128,128]{2,1,0:T(8,128)S(1)} pad(f32[65,128,128]{2,1,0:T(8,128)} %bitcast.341, f32[]{:T(128)} %constant.58.clone.1), padding=0_7x0_0x0_0 | pad | bytes 8978436
  96.0 4.8 %copy.22 = f32[9,8,128,128]{3,1,2,0:T(8,128)} copy(f32[9,8,128,128]{3,2,1,0:T(8,128)S(1)} %bitcast.340) | data formatting | bytes 9437184
  101.1 2.6 broadcast.29.clone2
  103.7 37.8 %while.43 = (s32[]{:T(128)}, f32[5,13,128,128]{3,2,1,0:T(8,128)}, s32[5]{0:T(128)S(1)}, bf16[128,2112]{1,0:T(8,128)(2,1)S(1)}, bf16[128,2048]{1,0:T(8,128)(2,1)S...) while((s32[]{:T(128)}, f32[5,13,128,128]{3,2,1,0:T(8,128)}, ...), condition=%wide.region_9.10_spmd, body=%wide.region_8.9_spmd.sunk | while | flops 872415232 | bytes 17892284 | solution.py:42
  110.2 1.0 constant_dynamic-update-slice_fusion.5
  117.8 1.0 constant_dynamic-update-slice_fusion.5
  125.3 1.0 constant_dynamic-update-slice_fusion.5
  132.9 1.0 constant_dynamic-update-slice_fusion.5
  140.5 1.0 constant_dynamic-update-slice_fusion.5
  141.5 3.1 %pad.13 = f32[72,128,128]{2,1,0:T(8,128)S(1)} pad(f32[65,128,128]{2,1,0:T(8,128)} %bitcast.342, f32[]{:T(128)} %constant.58.clone.1), padding=0_7x0_0x0_0 | pad | bytes 8978436
  144.6 2.7 copy.23
  147.4 2.6 multiply_convert_fusion
  150.1 23.3 %while.45 = (s32[]{:T(128)}, f32[65,256]{1,0:T(8,128)S(1)}, s32[8]{0:T(128)S(1)}, bf16[65,16384]{1,0:T(8,128)(2,1)}, s32[16384]{0:T(1024)S(1)}, /*index=5*/s32[]{:T(128)}, s32[1]{0:T(128)}, s32[]{:T(128)}, s32[]{:T(128)}) while((s32[]{:T(128)}, f32[65,256]{1,0:T(8,128)S(1)}, s32[8]{0:T(128)S(1)}, bf16[65,16384]{1,0:T(8,128)(2,1)}, ...), condition=%wide.region_11.12_spmd.clone, body=%wide.region_10.11_spmd.clone.sunk | while | flops 68715016 | bytes 452777 | solution.py:58
  151.4 1.5 fusion.281
  153.0 0.7 dynamic_slice.56
  154.4 1.5 fusion.281
  155.9 0.7 dynamic_slice.56
  157.3 1.5 fusion.281
  158.8 0.7 dynamic_slice.56
  160.2 1.5 fusion.281
  161.8 0.7 dynamic_slice.56
  163.1 1.5 fusion.281
  164.7 0.7 dynamic_slice.56
  166.0 1.5 fusion.281
  167.6 0.7 dynamic_slice.56
  169.0 1.5 fusion.281
  170.5 0.7 dynamic_slice.56
  171.9 1.5 fusion.281
  173.4 15.2 %while.44 = (s32[]{:T(128)}, f32[65,256]{1,0:T(8,128)S(1)}, s32[8]{0:T(128)S(1)}, bf16[65,16384]{1,0:T(8,128)(2,1)S(1)}, s32[16384]{0:T(1024)S(1)}, /*index=5*/s32[]{:T(128)}, s32[1]{0:T(128)}, s32[]{:T(128)}, s32[]{:T(128)}) while((s32[]{:T(128)}, f32[65,256]{1,0:T(8,128)S(1)}, s32[8]{0:T(128)S(1)}, ...), condition=%wide.region_7.8_spmd.clone, body=%wide.region_6.7_spmd.clone.sunk | while | flops 68715016 | bytes 459945 | solution.py:58
  173.5 0.7 dynamic_slice.53
  188.7 0.8 copy.13
  189.5 73.5 %reduce-scatter.4.cloned.1.call-done = f32[32,65]{1,0:T(8,128)} async-done(((f32[256,65]{1,0:T(8,128)}), f32[32,65]{1,0:T(8,128)}) %reduce-scatter.4.cloned.1.call-update) | async-done | bytes 8336
  263.0 0.8 copy.14
  263.8 10.5 %psum.16 = f32[65,32]{1,0:T(8,128)S(1)} all-reduce(f32[65,32]{1,0:T(8,128)S(1)} %copy.14), channel_id=1, replica_groups=mesh['chan'=8,'seg'=4] {'seg'}, use_global_device_ids=true, to_apply=%region_12.13 | all-reduce | flops 2080 | bytes 16640 | tf_op jit(solution)/shard_map/psum | solution.py:82
  274.3 0.7 copy.12
  (213 shorter events, 69.8 us)
Async XLA Ops:
  6.5 48.5 %copy-start = (bf16[128,2048]{1,0:T(8,128)(2,1)S(1)}, bf16[128,2048]{1,0:T(8,128)(2,1)}, u32[]{:S(2)}) copy-start(bf16[128,2048]{1,0:T(8,128)(2,1)} %param.10) | copy-start | bytes 1572868
  6.5 256.5 %reduce-scatter.4.cloned.1.call-start = ((), (), s32[]{:S(2)}) async-start(), calls=%async_computation.1 | async-start | bytes 147456
  6.5 39.6 %collective-permute-start = (bf16[128,2048]{1,0:T(8,128)(2,1)}, bf16[128,2048]{1,0:T(8,128)(2,1)S(1)}, u32[]{:S(2)}, u32[]{:S(2)}) collective-permute-start(bf16[128,2048]{1,0:T(8,128)(2,1)} %param.10), channel_id=1, source_target_pairs={{16,0},{20,4},{24,8},{28,12},{0,16},{4,20},{8,24},{12,28},{17,1},{... | collective-permute-start | bytes 1572872 | tf_op jit(solution)/shard_map/ppermute | solution.py:20
  10.6 35.7 %collective-permute-start.1 = (bf16[128,2048]{1,0:T(8,128)(2,1)}, bf16[128,2048]{1,0:T(8,128)(2,1)S(1)}, u32[]{:S(2)}, u32[]{:S(2)}) collective-permute-start(bf16[128,2048]{1,0:T(8,128)(2,1)} %param.10), channel_id=1, source_target_pairs={{12,0},{16,4},{20,8},{24,12},{28,16},{0,20},{4,24},{8,28},{13,1},{... | collective-permute-start | bytes 1572872 | tf_op jit(solution)/shard_map/ppermute | solution.py:20
  141.5 5.9 %slice-start = ((s8[4718592]{0:T(1024)(128)(4,1)}), s8[4194304]{0:T(1024)(128)(4,1)S(1)}, s32[]{:S(2)}) async-start(s8[4718592]{0:T(1024)(128)(4,1)} %bitcast.335), calls=%async_computation.2 | async-start | bytes 8388608
  144.6 2.8 slice-start.1
  147.4 2.7 copy-start.2
  150.1 23.4 %copy-start.1 = (f32[65,256]{1,0:T(8,128)S(1)}, f32[65,256]{1,0:T(8,128)}, u32[]{:S(2)}) copy-start(f32[65,256]{1,0:T(8,128)} %custom-call) | copy-start | bytes 199684
Sparse Core Ops, SparseCore 0:
  189.6 73.3 reduce-scatter.3
where the time goes:
time: 283 us; the launch traced here: 282 us
  waiting for transfers between devices  106 us (37%)
  matrix products  66.7 us (24%)
  local copies, waits for them, and re-layouts  51.9 us (18%)
  loops' own time  18.2 us (6%)
  blocking collectives  16.1 us (6%)
  between operations  13.6 us (5%)
  starting transfers between devices  5.36 us (2%)
  other arithmetic  4.33 us (2%)
    unnamed x2, waiting for transfers between devices  73.5 us
    dot_general x130, matrix products, lag_block(): lax.dot_general(own_block, shifted, (((1,), (1,)), ((), ())), preferred_e...  49.9 us
    ppermute x2, waiting for transfers between devices, from_behind(): return lax.ppermute(block, axis, route)  32.1 us
    dot_general x16, matrix products, bin_step(): jnp.dot(score_piece, onehot, preferred_element_type=jnp.float32)  16.8 us
    unnamed x16, local copies, waits for them, and re-layouts  15.2 us
    dynamic_update_slice x20, local copies, waits for them, and re-layouts, round_stack(): lax.scan(lag_block, 0, jnp.arange(lag_count // LAG_GROUP, dtype=jnp.int32))  12.9 us
    another operation x2, loops' own time, round_stack(): lax.scan(bin_step, running, jnp.arange(channels // row_block, dtype=jnp.i...  11.2 us
    psum x1, blocking collectives, local(): summed = lax.psum(partial_value, 'seg')  10.5 us
  transfers between devices with their start and end apart: 3, of which 2 were waited for; matrix products, arithmetic and copies ran while one was open for 1% of the time, Pallas kernels for 0%

commit v1 on v0

v1 whole, which is shorter than its diff:
```python
import functools
import math

import jax
import jax.numpy as jnp
from jax import lax
from jax.experimental import pallas as pl
from jax.experimental.pallas import tpu as pltpu
from jax.sharding import PartitionSpec as P

MAX_LAG = 32
NB = 256
ROUNDS = 2
LAGS = 2 * MAX_LAG + 1
EPSILON = 1e-06

FINE = 8
COARSE = MAX_LAG // FINE
LANES = 128
MESH = pl.DeviceIdType.MESH
CONTRACT = (((1,), (1,)), ((), ()))


def from_behind(block, axis, distance):
    devices = range(lax.axis_size(axis))
    route = [((i - distance) % len(devices), i) for i in devices]
    return lax.ppermute(block, axis, route)


def own_shifts(own):
    channels, length = own.shape
    padded = jnp.pad(own, ((0, 0), (FINE, FINE)))
    sides = []
    for first in (-FINE, 0):
        rows = [lax.slice_in_dim(padded, FINE - s, FINE - s + length, axis=1) for s in range(first, first + FINE)]
        sides.append(jnp.stack(rows, 1).reshape(channels * FINE, length))
    return sides


def partner_shifts(partner):
    length = partner.shape[1]
    padded = jnp.pad(partner, ((0, 0), (MAX_LAG, MAX_LAG)))
    starts = range(FINE, 2 * MAX_LAG + 1, FINE)
    return jnp.concatenate([lax.slice_in_dim(padded, start, start + length, axis=1) for start in starts], 0)


def stack_kernel(group, minus_ref, plus_ref, own_ref, partner_ref, scale_ref, bins_ref, out_ref, neg, pos, last, total):
    channels = own_ref.shape[0]
    width = partner_ref.shape[0] // (2 * COARSE)
    step = pl.program_id(0)

    @pl.when(step == 0)
    def _():
        total[...] = jnp.zeros_like(total)

    def dot(left, right):
        return lax.dot_general(left, right, CONTRACT, preferred_element_type=jnp.float32)

    neg[...] = dot(minus_ref[...], partner_ref[: COARSE * width])
    pos[...] = dot(plus_ref[...], partner_ref[(COARSE - 1) * width : (2 * COARSE - 1) * width])
    last[...] = dot(own_ref[...], partner_ref[(2 * COARSE - 1) * width :])

    bin_ids = lax.broadcasted_iota(jnp.int32, (NB, width), 0)

    @pl.loop(0, channels // group)
    def _(g):
        base = pl.multiple_of(g * group, group)
        scale = scale_ref[pl.ds(base, group), :]
        bins = bins_ref[pl.ds(base, group), :]
        top = last[pl.ds(base, group), :]
        scores, hots = [], []
        for a in range(group):
            rows = pl.ds(pl.multiple_of((base + a) * FINE, FINE), FINE)
            factor = jnp.broadcast_to(scale[a : a + 1], (FINE, width))
            pieces = []
            for side in (neg, pos):
                for k in range(COARSE):
                    pieces.append(side[rows, k * width : (k + 1) * width] * factor)
            edge = jnp.broadcast_to(top[a : a + 1], (FINE, width)) * factor
            pieces += [edge, edge]
            scores.append(jnp.concatenate(pieces, 0).astype(jnp.bfloat16))
            hit = jnp.broadcast_to(bins[a : a + 1], (NB, width)) == bin_ids
            hots.append(jnp.where(hit, 1.0, 0.0).astype(jnp.bfloat16))
        total[...] += dot(jnp.concatenate(scores, 1), jnp.concatenate(hots, 1))

    @pl.when(step == pl.num_programs(0) - 1)
    def _():
        out_ref[...] = total[...]


def round_stack(minus, plus, own, shifted, scale, bins):
    channels, length = own.shape
    step = channels // 2
    lag_rows = 2 * MAX_LAG + 2 * FINE
    fixed = lambda i: (0, 0)
    moving = lambda i: (i, 0)
    return pl.pallas_call(
        functools.partial(stack_kernel, 8),
        out_shape=jax.ShapeDtypeStruct((lag_rows, NB), jnp.float32),
        grid=(channels // step,),
        in_specs=[
            pl.BlockSpec((step * FINE, length), moving),
            pl.BlockSpec((step * FINE, length), moving),
            pl.BlockSpec((step, length), moving),
            pl.BlockSpec(shifted.shape, fixed),
            pl.BlockSpec((step, channels), moving),
            pl.BlockSpec((step, channels), moving),
        ],
        out_specs=pl.BlockSpec((lag_rows, NB), fixed),
        scratch_shapes=[
            pltpu.VMEM((step * FINE, COARSE * channels), jnp.float32),
            pltpu.VMEM((step * FINE, COARSE * channels), jnp.float32),
            pltpu.VMEM((step, channels), jnp.float32),
            pltpu.VMEM((lag_rows, NB), jnp.float32),
        ],
        compiler_params=pltpu.CompilerParams(vmem_limit_bytes=48 * 1024 * 1024),
        cost_estimate=pl.CostEstimate(
            flops=2 * LAGS * channels * channels * length,
            bytes_accessed=4 * channels * FINE * length * 2,
            transcendentals=0,
        ),
    )(minus, plus, own, shifted, scale, bins)


def reduce_kernel(n_chan, n_seg, part_ref, out_ref, arrived, mine, others, send1, recv1, send2, recv2):
    chan, seg = lax.axis_index("chan"), lax.axis_index("seg")
    rows = out_ref.shape[0]
    chan_peers = [lax.rem(chan + k, n_chan) for k in range(1, n_chan)]
    seg_peers = [lax.rem(seg + k, n_seg) for k in range(1, n_seg)]
    barrier = pltpu.get_barrier_semaphore()
    for peer in chan_peers:
        pl.semaphore_signal(barrier, inc=1, device_id=(peer, seg), device_id_type=MESH)
    for peer in seg_peers:
        pl.semaphore_signal(barrier, inc=1, device_id=(chan, peer), device_id_type=MESH)
    pl.semaphore_wait(barrier, n_chan + n_seg - 2)

    first = []
    for k, peer in enumerate(chan_peers):
        copy = pltpu.make_async_remote_copy(
            src_ref=part_ref.at[pl.ds(pl.multiple_of(peer * rows, rows), rows)],
            dst_ref=arrived.at[k],
            send_sem=send1.at[k],
            recv_sem=recv1.at[k],
            device_id=(peer, seg),
            device_id_type=MESH,
        )
        copy.start()
        first.append(copy)
    running = part_ref[pl.ds(pl.multiple_of(chan * rows, rows), rows), :]
    for k, copy in enumerate(first):
        copy.wait()
        running = running + arrived[k]
    mine[...] = running
    second = []
    for k, peer in enumerate(seg_peers):
        copy = pltpu.make_async_remote_copy(
            src_ref=mine,
            dst_ref=others.at[k],
            send_sem=send2.at[k],
            recv_sem=recv2.at[k],
            device_id=(chan, peer),
            device_id_type=MESH,
        )
        copy.start()
        second.append(copy)
    for copy in second:
        copy.wait()
    for position in range(n_seg):
        slot = lax.rem(seg - position + n_seg - 1 + n_seg, n_seg)
        term = jnp.where(slot == n_seg - 1, running, others[jnp.minimum(slot, n_seg - 2)])
        sums = term if position == 0 else sums + term
    out_ref[...] = sums


def reduce_all(part):
    n_chan, n_seg = lax.axis_size("chan"), lax.axis_size("seg")
    rows = part.shape[0] // n_chan
    block = (rows, part.shape[1])
    return pl.pallas_call(
        functools.partial(reduce_kernel, n_chan, n_seg),
        out_shape=jax.ShapeDtypeStruct(block, jnp.float32),
        in_specs=[pl.BlockSpec(memory_space=pltpu.VMEM)],
        out_specs=pl.BlockSpec(memory_space=pltpu.VMEM),
        scratch_shapes=[
            pltpu.VMEM((n_chan - 1,) + block, jnp.float32),
            pltpu.VMEM(block, jnp.float32),
            pltpu.VMEM((n_seg - 1,) + block, jnp.float32),
            pltpu.SemaphoreType.DMA((n_chan - 1,)),
            pltpu.SemaphoreType.DMA((n_chan - 1,)),
            pltpu.SemaphoreType.DMA((n_seg - 1,)),
            pltpu.SemaphoreType.DMA((n_seg - 1,)),
        ],
        compiler_params=pltpu.CompilerParams(
            collective_id=0, has_side_effects=True, vmem_limit_bytes=16 * 1024 * 1024
        ),
    )(part)


def local(traces, pair_bins):
    channels, seg_length = traces.shape
    chan_count = lax.axis_size("chan")
    seg_count = lax.axis_size("seg")
    total_time = seg_length * seg_count
    time_scale = 1.0 / math.sqrt(total_time)
    half_loop = chan_count // 2
    far_block = from_behind(traces, "chan", -half_loop)
    near_block = from_behind(traces, "chan", 1 - half_loop)
    energy = lax.psum(jnp.sum(jnp.square(traces.astype(jnp.float32)), axis=1), "seg")
    scale = lax.rsqrt(energy / total_time + EPSILON)
    far_scale = from_behind(scale, "chan", -half_loop)
    near_scale = from_behind(scale, "chan", 1 - half_loop)
    minus, plus = own_shifts(traces)

    def partial_stack(block, block_scale, bins):
        pair_scale = scale[:, None] * block_scale[None, :] * time_scale
        return round_stack(minus, plus, traces, partner_shifts(block), pair_scale, bins)

    part = partial_stack(far_block, far_scale, pair_bins[0])
    part = part + partial_stack(near_block, near_scale, pair_bins[1])
    pair_total = ROUNDS * chan_count * channels * channels // NB
    part = part.T * (1.0 / math.sqrt(pair_total))
    part = jnp.pad(part, ((0, 0), (0, -part.shape[1] % LANES)))
    return reduce_all(part).T[:LAGS]


def solution(mesh):
    in_specs = (P("chan", "seg"), P(None, "chan", None))
    out_specs = P(None, "chan")
    return jax.shard_map(local, mesh=mesh, in_specs=in_specs, out_specs=out_specs, check_vma=False)
```

time: 283 us -> 83.6 us (0.30)
  waiting for transfers between devices: 106 us -> 8.81 us
  matrix products: 66.7 us -> 0 us
  Pallas kernels: 0 us -> 35.6 us
  local copies, waits for them, and re-layouts: 51.9 us -> 21.6 us
  loops' own time: 18.2 us -> 0 us
  between operations: 13.6 us -> 0.34 us
  blocking collectives: 16.1 us -> 6.59 us
  starting transfers between devices: 5.36 us -> 9.03 us
  other arithmetic: 4.33 us -> 1.38 us
    unnamed x2 -> x0, waiting for transfers between devices: 73.5 us -> none
    dot_general x146 -> x0, matrix products: 66.7 us -> none  [the longest x130 49.9 us: lag_block(): lax.dot_general(own_block, shifted, (((1,), (1,)), ((), ())), preferred_e...]
    pallas_call x0 -> x3, Pallas kernels: none -> 35.6 us  [the longest x2 25.3 us: round_stack(): pl.pallas_call(functools.partial(stack_kernel, 8), out_shape=jax.ShapeDty...]
    ppermute x2 -> x4, waiting for transfers between devices: 32.1 us -> 8.81 us  [from_behind(): return lax.ppermute(block, axis, route)]
    another operation x4 -> x0, loops' own time: 18.2 us -> none  [the longest x2 11.2 us: round_stack(): lax.scan(bin_step, running, jnp.arange(channels // row_block, dtype=jnp.i...]
    dynamic_slice x42 -> x0, local copies, waits for them, and re-layouts: 16.6 us -> none  [the longest x16 10.4 us: round_stack(): lax.scan(bin_step, running, jnp.arange(channels // row_block, dtype=jnp.i...]
    dynamic_update_slice x20 -> x0, local copies, waits for them, and re-layouts: 12.9 us -> none  [round_stack(): lax.scan(lag_block, 0, jnp.arange(lag_count // LAG_GROUP, dtype=jnp.int32))]
    psum x2 -> x1, blocking collectives: 16.1 us -> 6.59 us  [local(): lax.psum(jnp.sum(jnp.square(traces.astype(jnp.float32)), axis=1), 'seg')]
  transfers between devices with their start and end apart: 3 -> 4, of which waited for: 2 -> 1; matrix products, arithmetic and copies ran while one was open for 1% -> 20% of each run, Pallas kernels for 0% -> 15%
where the time goes in v1:
time: 83.6 us; the launch traced here: 83.3 us
  Pallas kernels  35.6 us (43%)
  local copies, waits for them, and re-layouts  21.6 us (26%)
  starting transfers between devices  9.03 us (11%)
  waiting for transfers between devices  8.81 us (11%)
  blocking collectives  6.59 us (8%)
  other arithmetic  1.38 us (2%)
    pallas_call x2, Pallas kernels, round_stack(): pl.pallas_call(functools.partial(stack_kernel, 8), out_shape=jax.ShapeDty...  25.3 us
    unnamed x35, local copies, waits for them, and re-layouts  13.9 us
    pallas_call x1, Pallas kernels, reduce_all(): pl.pallas_call(functools.partial(reduce_kernel, n_chan, n_seg), out_shape...  10.3 us
    ppermute x4, starting transfers between devices, from_behind(): return lax.ppermute(block, axis, route)  9.03 us
    ppermute x4, waiting for transfers between devices, from_behind(): return lax.ppermute(block, axis, route)  8.81 us
    another operation x4, local copies, waits for them, and re-layouts, own_shifts(): sides.append(jnp.stack(rows, 1).reshape(channels * FINE, length))  7.13 us
    psum x1, blocking collectives, local(): lax.psum(jnp.sum(jnp.square(traces.astype(jnp.float32)), axis=1), 'seg')  6.59 us
  transfers between devices with their start and end apart: 4, of which 1 were waited for; matrix products, arithmetic and copies ran while one was open for 20% of the time, Pallas kernels for 15%

profile of v1, /device:TPU:0, one launch (start us, length us, event | category | flops | bytes accessed | tf_op | source)
XLA Modules:
  0.0 83.3 jit_solution(17590355808647143541)
XLA Ops:
  0.0 4.1 %collective-permute-start = (bf16[128,2048]{1,0:T(8,128)(2,1)}, bf16[128,2048]{1,0:T(8,128)(2,1)S(1)}, u32[]{:S(2)}, u32[]{:S(2)}) collective-permute-start(bf16[128,2048]{1,0:T(8,128)(2,1)} %own_ref.3), channel_id=1, source_target_pairs={{16,0},{20,4},{24,8},{28,12},{0,16},{4,20},{8,24},{12,28},{17,1},{... | collective-permute-start | bytes 1572872 | tf_op jit(solution)/shard_map/ppermute | solution.py:27
  4.1 1.3 %multiply_reduce_fusion = f32[128]{0:T(128)S(1)} fusion(bf16[128,2048]{1,0:T(8,128)(2,1)} %own_ref.3), kind=kLoop, calls=%fused_computation.2 | loop fusion | flops 786304 | bytes 524800 | tf_op jit(solution)/shard_map/reduce_sum | solution.py:208
  5.3 6.6 %psum.7 = f32[128]{0:T(128)S(1)} all-reduce(f32[128]{0:T(128)S(1)} %multiply_reduce_fusion), channel_id=1, replica_groups=mesh['chan'=8,'seg'=4] {'seg'}, use_global_device_ids=true, to_apply=%region_1.0 | all-reduce | flops 128 | bytes 1024 | tf_op jit(solution)/shard_map/psum | solution.py:208
  11.9 1.4 %collective-permute-start.3 = (f32[128]{0:T(128)S(1)}, f32[128]{0:T(128)S(1)}, u32[]{:S(2)}, u32[]{:S(2)}) collective-permute-start(f32[128]{0:T(128)S(1)} %add_rsqrt_fusion), channel_id=1, source_target_pairs={{12,0},{16,4},{20,8},{24,12},{28,16},{0,20},{4,24},{8,28},{13,1},{... | collective-permute-start | bytes 1544 | tf_op jit(solution)/shard_map/ppermute | solution.py:27
  13.3 2.5 %collective-permute-start.1 = (f32[128]{0:T(128)S(1)}, f32[128]{0:T(128)S(1)}, u32[]{:S(2)}, u32[]{:S(2)}) collective-permute-start(f32[128]{0:T(128)S(1)} %add_rsqrt_fusion), channel_id=1, source_target_pairs={{16,0},{20,4},{24,8},{28,12},{0,16},{4,20},{8,24},{12,28},{17,1},{... | collective-permute-start | bytes 1544 | tf_op jit(solution)/shard_map/ppermute | solution.py:27
  15.8 1.1 %collective-permute-start.2 = (bf16[128,2048]{1,0:T(8,128)(2,1)}, bf16[128,2048]{1,0:T(8,128)(2,1)S(1)}, u32[]{:S(2)}, u32[]{:S(2)}) collective-permute-start(bf16[128,2048]{1,0:T(8,128)(2,1)} %own_ref.3), channel_id=1, source_target_pairs={{12,0},{16,4},{20,8},{24,12},{28,16},{0,20},{4,24},{8,28},{13,1},{... | collective-permute-start | bytes 1572872 | tf_op jit(solution)/shard_map/ppermute | solution.py:27
  16.9 1.1 %bitcast_dynamic-update-slice_fusion.7 = bf16[128,8,2048]{2,0,1:T(8,128)(2,1)S(1)} fusion(bf16[128,2048]{1,0:T(8,128)(2,1)} %own_ref.3), kind=kLoop, calls=%fused_computation.10 | loop fusion | bytes 1048576
  18.0 1.3 %bitcast_dynamic-update-slice_fusion.6 = bf16[128,8,2048]{2,0,1:T(8,128)(2,1)S(1)} fusion(bf16[128,8,2048]{2,0,1:T(8,128)(2,1)S(1)} %bitcast_dynamic-update-slice_fusion.7, bf16[128,2048]{1,0:T(8,128)(2,1)} %own_ref.3), kind=kLoop, calls=%fused_computation.9 | loop fusion | bytes 1048576
  19.3 1.3 %bitcast_dynamic-update-slice_fusion.5 = bf16[128,8,2048]{2,0,1:T(8,128)(2,1)S(1)} fusion(bf16[128,8,2048]{2,0,1:T(8,128)(2,1)S(1)} %bitcast_dynamic-update-slice_fusion.6, bf16[128,2048]{1,0:T(8,128)(2,1)} %own_ref.3), kind=kLoop, calls=%fused_computation.8 | loop fusion | bytes 1048576
  20.5 1.3 %bitcast_dynamic-update-slice_fusion.4 = bf16[128,8,2048]{2,0,1:T(8,128)(2,1)S(1)} fusion(bf16[128,8,2048]{2,0,1:T(8,128)(2,1)S(1)} %bitcast_dynamic-update-slice_fusion.5, bf16[128,2048]{1,0:T(8,128)(2,1)} %own_ref.3), kind=kLoop, calls=%fused_computation.7 | loop fusion | bytes 1048576
  21.8 0.2 bitcast_dynamic-update-slice_fusion.3
  22.0 0.2 bitcast_dynamic-update-slice_fusion.2
  22.2 0.4 bitcast_dynamic-update-slice_fusion.1
  22.6 0.0 copy-start.1
  22.6 0.4 bitcast_dynamic-update-slice_fusion
  23.0 0.2 bitcast_dynamic-update-slice_fusion.13
  23.3 0.2 bitcast_dynamic-update-slice_fusion.12
  23.5 0.2 bitcast_dynamic-update-slice_fusion.11
  23.7 0.2 bitcast_dynamic-update-slice_fusion.10
  23.9 0.2 bitcast_dynamic-update-slice_fusion.9
  24.1 0.2 bitcast_dynamic-update-slice_fusion.8
  24.4 2.3 %copy.13 = bf16[128,8,2048]{2,1,0:T(8,128)(2,1)S(1)} copy(bf16[128,8,2048]{2,0,1:T(8,128)(2,1)S(1)} %bitcast_dynamic-update-slice_fusion.8) | data formatting | bytes 8388608 | tf_op jit(solution)/shard_map/stack | solution.py:36
  26.7 4.2 %copy.12 = bf16[128,8,2048]{2,1,0:T(8,128)(2,1)} copy(bf16[128,8,2048]{2,0,1:T(8,128)(2,1)S(1)} %get-tuple-element.5) | data formatting | bytes 8388608 | tf_op jit(solution)/shard_map/stack | solution.py:36
  30.9 0.0 collective-permute-done.3
  30.9 8.8 %collective-permute-done.1 = f32[128]{0:T(128)S(1)} collective-permute-done((f32[128]{0:T(128)S(1)}, f32[128]{0:T(128)S(1)}, u32[]{:S(2)}, u32[]{:S(2)}) %collective-permute-start.1) | collective-permute-done | bytes 544 | tf_op jit(solution)/shard_map/ppermute | solution.py:27
  39.7 0.1 multiply_multiply_fusion
  39.8 0.2 slice_dynamic-update-slice_fusion.13
  40.0 0.2 slice_dynamic-update-slice_fusion.12
  40.3 0.2 slice_dynamic-update-slice_fusion.11
  40.5 0.2 slice_dynamic-update-slice_fusion.10
  40.7 0.2 slice_dynamic-update-slice_fusion.9
  41.0 0.2 slice_dynamic-update-slice_fusion.8
  41.2 0.2 slice_dynamic-update-slice_fusion.7.partner_ref
  41.4 2.0 %copy-done.2 = bf16[1024,2048]{1,0:T(8,128)(2,1)} copy-done((bf16[1024,2048]{1,0:T(8,128)(2,1)}, bf16[1024,2048]{1,0:T(8,128)(2,1)S(1)}, u32[]{:S(2)}) %copy-start.2) | copy-done | bytes 4194328
  43.4 12.7 %shard_map.28 = f32[80,256]{1,0:T(8,128)S(1)} custom-call(bf16[1024,2048]{1,0:T(8,128)(2,1)S(1)} %bitcast.46, bf16[1024,2048]{1,0:T(8,128)(2,1)} %bitcast.49, bf16[128,2048]{1,0:T(8,128)(2,1)S(1)} %copy-done, bf16[1024,2048]{1,0:T(8,128)(2,1)} %copy-done.2, f32[128,128]{1,0:T(8,128)S(1)} %get-tuple-element.12.scale_ref, ...), custom_call_target="tpu_custom_call" | custom-call | flops 4362076160 | bytes 16777216 | tf_op jit(solution)/shard_map/pallas_call | solution.py:97
  56.0 0.0 collective-permute-done.2
  56.0 0.2 slice_dynamic-update-slice_fusion.6
  56.3 0.2 slice_dynamic-update-slice_fusion.5
  56.5 0.2 slice_dynamic-update-slice_fusion.4
  56.7 0.2 slice_dynamic-update-slice_fusion.3
  57.0 0.2 slice_dynamic-update-slice_fusion.2
  57.2 0.2 slice_dynamic-update-slice_fusion.1
  57.4 0.2 slice_dynamic-update-slice_fusion.partner_ref
  57.6 2.0 %copy-done.3 = bf16[1024,2048]{1,0:T(8,128)(2,1)} copy-done((bf16[1024,2048]{1,0:T(8,128)(2,1)}, bf16[1024,2048]{1,0:T(8,128)(2,1)S(1)}, u32[]{:S(2)}) %copy-start.3) | copy-done | bytes 4194328
  59.6 12.7 %shard_map.29 = f32[80,256]{1,0:T(8,128)S(1)} custom-call(bf16[1024,2048]{1,0:T(8,128)(2,1)S(1)} %bitcast.47, bf16[1024,2048]{1,0:T(8,128)(2,1)} %bitcast.50, bf16[128,2048]{1,0:T(8,128)(2,1)S(1)} %copy-done, bf16[1024,2048]{1,0:T(8,128)(2,1)} %copy-done.3, f32[128,128]{1,0:T(8,128)S(1)} %get-tuple-element.11.scale_ref, s32[128,128]{1,0:T(8,128)S(1)} %get-tuple-element.9.bins_ref), custom_call_target="tpu_custom_call" | custom-call | flops 4362076160 | bytes 16777216 | tf_op jit(solution)/shard_map/pallas_call | solution.py:97
  72.3 0.1 copy.9
  72.4 10.3 %shard_map.30 = f32[32,128]{1,0:T(8,128)S(1)} custom-call(f32[256,128]{1,0:T(8,128)S(1)} %pad.18.part_ref), custom_call_target="tpu_custom_call" | custom-call | tf_op jit(solution)/shard_map/pallas_call | solution.py:179
  82.7 0.6 copy.43
  (13 shorter events, 0.1 us)
Async XLA Ops:
  0.0 21.8 %copy-start = (bf16[128,2048]{1,0:T(8,128)(2,1)S(1)}, bf16[128,2048]{1,0:T(8,128)(2,1)}, u32[]{:S(2)}) copy-start(bf16[128,2048]{1,0:T(8,128)(2,1)} %own_ref.3) | copy-start | bytes 1572868
  0.0 39.8 %collective-permute-start = (bf16[128,2048]{1,0:T(8,128)(2,1)}, bf16[128,2048]{1,0:T(8,128)(2,1)S(1)}, u32[]{:S(2)}, u32[]{:S(2)}) collective-permute-start(bf16[128,2048]{1,0:T(8,128)(2,1)} %own_ref.3), channel_id=1, source_target_pairs={{16,0},{20,4},{24,8},{28,12},{0,16},{4,20},{8,24},{12,28},{17,1},{... | collective-permute-start | bytes 1572872 | tf_op jit(solution)/shard_map/ppermute | solution.py:27
  11.9 19.0 %collective-permute-start.3 = (f32[128]{0:T(128)S(1)}, f32[128]{0:T(128)S(1)}, u32[]{:S(2)}, u32[]{:S(2)}) collective-permute-start(f32[128]{0:T(128)S(1)} %add_rsqrt_fusion), channel_id=1, source_target_pairs={{12,0},{16,4},{20,8},{24,12},{28,16},{0,20},{4,24},{8,28},{13,1},{... | collective-permute-start | bytes 1544 | tf_op jit(solution)/shard_map/ppermute | solution.py:27
  13.3 26.4 %collective-permute-start.1 = (f32[128]{0:T(128)S(1)}, f32[128]{0:T(128)S(1)}, u32[]{:S(2)}, u32[]{:S(2)}) collective-permute-start(f32[128]{0:T(128)S(1)} %add_rsqrt_fusion), channel_id=1, source_target_pairs={{16,0},{20,4},{24,8},{28,12},{0,16},{4,20},{8,24},{12,28},{17,1},{... | collective-permute-start | bytes 1544 | tf_op jit(solution)/shard_map/ppermute | solution.py:27
  15.8 40.2 %collective-permute-start.2 = (bf16[128,2048]{1,0:T(8,128)(2,1)}, bf16[128,2048]{1,0:T(8,128)(2,1)S(1)}, u32[]{:S(2)}, u32[]{:S(2)}) collective-permute-start(bf16[128,2048]{1,0:T(8,128)(2,1)} %own_ref.3), channel_id=1, source_target_pairs={{12,0},{16,4},{20,8},{24,12},{28,16},{0,20},{4,24},{8,28},{13,1},{... | collective-permute-start | bytes 1572872 | tf_op jit(solution)/shard_map/ppermute | solution.py:27
  22.6 1.7 %copy-start.1 = (s32[2,128,128]{2,1,0:T(8,128)S(1)}, s32[2,128,128]{2,1,0:T(8,128)}, u32[]{:S(2)}) copy-start(s32[2,128,128]{2,1,0:T(8,128)} %param.3) | copy-start | bytes 393220
  41.4 2.0 %copy-start.2 = (bf16[1024,2048]{1,0:T(8,128)(2,1)}, bf16[1024,2048]{1,0:T(8,128)(2,1)S(1)}, u32[]{:S(2)}) copy-start(bf16[1024,2048]{1,0:T(8,128)(2,1)S(1)} %slice_dynamic-update-slice_fusion.7.partner_ref) | copy-start | bytes 12582916
  57.6 2.0 %copy-start.3 = (bf16[1024,2048]{1,0:T(8,128)(2,1)}, bf16[1024,2048]{1,0:T(8,128)(2,1)S(1)}, u32[]{:S(2)}) copy-start(bf16[1024,2048]{1,0:T(8,128)(2,1)S(1)} %slice_dynamic-update-slice_fusion.partner_ref) | copy-start | bytes 12582916

commit v2 on v1

v2 whole, which is shorter than its diff:
```python
import functools
import math

import jax
import jax.numpy as jnp
from jax import lax
from jax.experimental import pallas as pl
from jax.experimental.pallas import tpu as pltpu
from jax.sharding import PartitionSpec as P

MAX_LAG = 32
NB = 256
ROUNDS = 2
LAGS = 2 * MAX_LAG + 1
EPSILON = 1e-06

FINE = 8
COARSE = MAX_LAG // FINE
LANES = 128
CHUNKS = 4
MESH = pl.DeviceIdType.MESH
CONTRACT = (((1,), (1,)), ((), ()))


def from_behind(block, axis, distance):
    devices = range(lax.axis_size(axis))
    route = [((i - distance) % len(devices), i) for i in devices]
    return lax.ppermute(block, axis, route)


def coarse_shifts(block):
    length = block.shape[1]
    padded = jnp.pad(block, ((0, 0), (MAX_LAG, MAX_LAG)))
    starts = range(FINE, 2 * MAX_LAG + 1, FINE)
    return jnp.concatenate([lax.slice_in_dim(padded, start, start + length, axis=1) for start in starts], 0)


def stack_kernel(group, first, far_ref, near_ref, scale_ref, bins_ref, prior_ref, out_ref, fine, neg, pos, last):
    channels, length = far_ref.shape
    width = near_ref.shape[0] // (2 * COARSE)

    def dot(left, right):
        return lax.dot_general(left, right, CONTRACT, preferred_element_type=jnp.float32)

    pair = 2
    tile = pair * FINE
    blank = jnp.zeros((FINE, LANES), jnp.float32)
    for block in range(channels // tile):
        wide = far_ref[block * tile : (block + 1) * tile, :].astype(jnp.float32)
        for start in range(0, tile, pair):
            both = []
            for x in range(start, start + pair):
                row = jnp.broadcast_to(wide[x : x + 1], (FINE, length))
                both.append(jnp.concatenate([row, blank], 1))
            rows = slice((block * tile + start) * FINE, (block * tile + start + pair) * FINE)
            for side, base in ((0, LANES + length - FINE), (1, 0)):
                turned = [pltpu.roll(row, base, 1, stride=1, stride_axis=0)[:, :length] for row in both]
                fine[side, rows, :] = jnp.concatenate(turned, 0).astype(jnp.bfloat16)

    neg[...] = dot(fine[0], near_ref[: COARSE * width])
    pos[...] = dot(fine[1], near_ref[(COARSE - 1) * width : (2 * COARSE - 1) * width])
    last[...] = dot(far_ref[...], near_ref[(2 * COARSE - 1) * width :])

    bin_ids = lax.broadcasted_iota(jnp.int32, (NB, width), 0)
    out_ref[...] = jnp.zeros_like(out_ref) if first else prior_ref[...]

    @pl.loop(0, channels // group)
    def _(g):
        base = pl.multiple_of(g * group, group)
        scale = scale_ref[pl.ds(base, group), :]
        bins = bins_ref[pl.ds(base, group), :]
        top = last[pl.ds(base, group), :]
        for half in range(0, group, group // 2):
            scores, hots = [], []
            for x in range(half, half + group // 2):
                rows = pl.ds(pl.multiple_of((base + x) * FINE, FINE), FINE)
                factor = jnp.broadcast_to(scale[x : x + 1], (FINE, width))
                pieces = []
                for side in (neg, pos):
                    for k in range(COARSE):
                        pieces.append(side[rows, k * width : (k + 1) * width] * factor)
                edge = jnp.broadcast_to(top[x : x + 1], (FINE, width)) * factor
                pieces += [edge, edge]
                scores.append(jnp.concatenate(pieces, 0).astype(jnp.bfloat16))
                hit = jnp.broadcast_to(bins[x : x + 1], (NB, width)) == bin_ids
                hots.append(jnp.where(hit, 1.0, 0.0).astype(jnp.bfloat16))
            out_ref[...] += dot(jnp.concatenate(scores, 1), jnp.concatenate(hots, 1))


def chunk_stack(far, near, scale, bins, prior):
    channels, length = far.shape
    width = near.shape[0] // (2 * COARSE)
    lag_rows = 2 * MAX_LAG + 2 * FINE
    first = prior is None
    if first:
        prior = jnp.zeros((8, LANES), jnp.float32)
    return pl.pallas_call(
        functools.partial(stack_kernel, 8, first),
        out_shape=jax.ShapeDtypeStruct((lag_rows, NB), jnp.float32),
        in_specs=[pl.BlockSpec(memory_space=pltpu.VMEM)] * 5,
        out_specs=pl.BlockSpec(memory_space=pltpu.VMEM),
        scratch_shapes=[
            pltpu.VMEM((2, channels * FINE, length), jnp.bfloat16),
            pltpu.VMEM((channels * FINE, COARSE * width), jnp.float32),
            pltpu.VMEM((channels * FINE, COARSE * width), jnp.float32),
            pltpu.VMEM((channels, width), jnp.float32),
        ],
        compiler_params=pltpu.CompilerParams(vmem_limit_bytes=32 * 1024 * 1024),
        cost_estimate=pl.CostEstimate(
            flops=2 * LAGS * channels * width * length, bytes_accessed=near.size * 2, transcendentals=0
        ),
    )(far, near, scale, bins, prior)


def reduce_kernel(n_chan, n_seg, part_ref, out_ref, arrived, mine, others, send1, recv1, send2, recv2):
    chan, seg = lax.axis_index("chan"), lax.axis_index("seg")
    rows = out_ref.shape[0]
    chan_peers = [lax.rem(chan + k, n_chan) for k in range(1, n_chan)]
    seg_peers = [lax.rem(seg + k, n_seg) for k in range(1, n_seg)]
    barrier = pltpu.get_barrier_semaphore()
    for peer in chan_peers:
        pl.semaphore_signal(barrier, inc=1, device_id=(peer, seg), device_id_type=MESH)
    for peer in seg_peers:
        pl.semaphore_signal(barrier, inc=1, device_id=(chan, peer), device_id_type=MESH)
    pl.semaphore_wait(barrier, n_chan + n_seg - 2)

    first = []
    for k, peer in enumerate(chan_peers):
        copy = pltpu.make_async_remote_copy(
            src_ref=part_ref.at[pl.ds(pl.multiple_of(peer * rows, rows), rows)],
            dst_ref=arrived.at[k],
            send_sem=send1.at[k],
            recv_sem=recv1.at[k],
            device_id=(peer, seg),
            device_id_type=MESH,
        )
        copy.start()
        first.append(copy)
    running = part_ref[pl.ds(pl.multiple_of(chan * rows, rows), rows), :]
    for k, copy in enumerate(first):
        copy.wait()
        running = running + arrived[k]
    mine[...] = running
    second = []
    for k, peer in enumerate(seg_peers):
        copy = pltpu.make_async_remote_copy(
            src_ref=mine,
            dst_ref=others.at[k],
            send_sem=send2.at[k],
            recv_sem=recv2.at[k],
            device_id=(chan, peer),
            device_id_type=MESH,
        )
        copy.start()
        second.append(copy)
    for copy in second:
        copy.wait()
    for position in range(n_seg):
        slot = lax.rem(seg - position + n_seg - 1 + n_seg, n_seg)
        term = jnp.where(slot == n_seg - 1, running, others[jnp.minimum(slot, n_seg - 2)])
        sums = term if position == 0 else sums + term
    out_ref[...] = sums


def reduce_all(part):
    n_chan, n_seg = lax.axis_size("chan"), lax.axis_size("seg")
    rows = part.shape[0] // n_chan
    block = (rows, part.shape[1])
    return pl.pallas_call(
        functools.partial(reduce_kernel, n_chan, n_seg),
        out_shape=jax.ShapeDtypeStruct(block, jnp.float32),
        in_specs=[pl.BlockSpec(memory_space=pltpu.VMEM)],
        out_specs=pl.BlockSpec(memory_space=pltpu.VMEM),
        scratch_shapes=[
            pltpu.VMEM((n_chan - 1,) + block, jnp.float32),
            pltpu.VMEM(block, jnp.float32),
            pltpu.VMEM((n_seg - 1,) + block, jnp.float32),
            pltpu.SemaphoreType.DMA((n_chan - 1,)),
            pltpu.SemaphoreType.DMA((n_chan - 1,)),
            pltpu.SemaphoreType.DMA((n_seg - 1,)),
            pltpu.SemaphoreType.DMA((n_seg - 1,)),
        ],
        compiler_params=pltpu.CompilerParams(
            collective_id=0, has_side_effects=True, vmem_limit_bytes=16 * 1024 * 1024
        ),
    )(part)


def local(traces, pair_bins):
    channels, seg_length = traces.shape
    chan_count = lax.axis_size("chan")
    seg_count = lax.axis_size("seg")
    total_time = seg_length * seg_count
    time_scale = 1.0 / math.sqrt(total_time)
    half_loop = chan_count // 2
    next_block = from_behind(traces, "chan", -1)
    next_bins = from_behind(pair_bins[1], "chan", -1)
    size = channels // CHUNKS
    far_chunks = [from_behind(traces[k * size : (k + 1) * size], "chan", -half_loop) for k in range(CHUNKS)]
    energy = lax.psum(jnp.sum(jnp.square(traces.astype(jnp.float32)), axis=1), "seg")
    scale = lax.rsqrt(energy / total_time + EPSILON)
    far_scale = from_behind(scale, "chan", -half_loop)
    next_scale = from_behind(scale, "chan", -1)
    near = coarse_shifts(jnp.concatenate([traces, next_block], 0))
    near_scale = jnp.concatenate([scale, next_scale], 0)
    pair_scale = far_scale[:, None] * near_scale[None, :] * time_scale
    bins = jnp.concatenate([pair_bins[0], next_bins], 0).T
    part = None
    for k, chunk in enumerate(far_chunks):
        rows = slice(k * size, (k + 1) * size)
        part = chunk_stack(chunk, near, pair_scale[rows], bins[rows], part)
    pair_total = ROUNDS * chan_count * channels * channels // NB
    part = part.T * (1.0 / math.sqrt(pair_total))
    part = jnp.pad(part, ((0, 0), (0, -part.shape[1] % LANES)))
    return reduce_all(part).T[:LAGS][::-1]


def solution(mesh):
    in_specs = (P("chan", "seg"), P(None, "chan", None))
    out_specs = P(None, "chan")
    return jax.shard_map(local, mesh=mesh, in_specs=in_specs, out_specs=out_specs, check_vma=False)
```

time: 83.6 us -> 64.4 us (0.77)
  local copies, waits for them, and re-layouts: 21.6 us -> 5.88 us
  Pallas kernels: 35.6 us -> 27.3 us
  starting transfers between devices: 9.03 us -> 14.5 us
  waiting for transfers between devices: 8.81 us -> 6.73 us
  other arithmetic: 1.38 us -> 2.85 us
    unnamed x35 -> x12, local copies, waits for them, and re-layouts: 13.9 us -> 2.67 us
    pallas_call x2 -> x4, Pallas kernels: 25.3 us -> 18 us  [chunk_stack(): pl.pallas_call(functools.partial(stack_kernel, 8, first), out_shape=jax.S...]
    another operation x4 -> x0, local copies, waits for them, and re-layouts: 7.13 us -> none  [own_shifts(): sides.append(jnp.stack(rows, 1).reshape(channels * FINE, length))]
    ppermute x4 -> x8, starting transfers between devices: 9.03 us -> 14.5 us  [from_behind(): return lax.ppermute(block, axis, route)]
    ppermute x4 -> x8, waiting for transfers between devices: 8.81 us -> 6.73 us  [from_behind(): return lax.ppermute(block, axis, route)]
    slice x0 -> x4, local copies, waits for them, and re-layouts: none -> 2.03 us  [the longest x1 1.13 us: local(): traces[k * size:(k + 1) * size]]
    concatenate x0 -> x2, other arithmetic: none -> 1.48 us  [the longest x1 1.47 us: local(): near = coarse_shifts(jnp.concatenate([traces, next_block], 0))]
    pallas_call x1, Pallas kernels: 10.3 us -> 9.28 us  [reduce_all(): pl.pallas_call(functools.partial(reduce_kernel, n_chan, n_seg), out_shape...]
  transfers between devices with their start and end apart: 4 -> 8, of which waited for: 1 -> 1; matrix products, arithmetic and copies ran while one was open for 20% -> 12% of each run, Pallas kernels for 15% -> 21%
where the time goes in v2:
time: 64.4 us; the launch traced here: 64.1 us
  Pallas kernels  27.3 us (42%)
  starting transfers between devices  14.5 us (23%)
  waiting for transfers between devices  6.73 us (10%)
  blocking collectives  6.59 us (10%)
  local copies, waits for them, and re-layouts  5.88 us (9%)
  other arithmetic  2.85 us (4%)
    pallas_call x4, Pallas kernels, chunk_stack(): pl.pallas_call(functools.partial(stack_kernel, 8, first), out_shape=jax.S...  18 us
    ppermute x8, starting transfers between devices, from_behind(): return lax.ppermute(block, axis, route)  14.5 us
    pallas_call x1, Pallas kernels, reduce_all(): pl.pallas_call(functools.partial(reduce_kernel, n_chan, n_seg), out_shape...  9.28 us
    ppermute x8, waiting for transfers between devices, from_behind(): return lax.ppermute(block, axis, route)  6.73 us
    psum x1, blocking collectives, local(): lax.psum(jnp.sum(jnp.square(traces.astype(jnp.float32)), axis=1), 'seg')  6.59 us
    unnamed x12, local copies, waits for them, and re-layouts  2.67 us
    concatenate x1, other arithmetic, local(): near = coarse_shifts(jnp.concatenate([traces, next_block], 0))  1.47 us
  transfers between devices with their start and end apart: 8, of which 1 were waited for; matrix products, arithmetic and copies ran while one was open for 12% of the time, Pallas kernels for 21%

profile of v2, /device:TPU:0, one launch (start us, length us, event | category | flops | bytes accessed | tf_op | source)
XLA Modules:
  0.0 64.1 jit_solution(1004223083836098320)
XLA Ops:
  0.0 0.0 copy-start
  0.0 6.0 %collective-permute-start.1 = (bf16[128,2048]{1,0:T(8,128)(2,1)}, bf16[128,2048]{1,0:T(8,128)(2,1)S(1)}, u32[]{:S(2)}, u32[]{:S(2)}) collective-permute-start(bf16[128,2048]{1,0:T(8,128)(2,1)} %param.2), channel_id=1, source_target_pairs={{4,0},{8,4},{12,8},{16,12},{20,16},{24,20},{28,24},{0,28},{5,1},{9... | collective-permute-start | bytes 1572872 | tf_op jit(solution)/shard_map/ppermute | solution.py:28
  6.0 1.3 %multiply_reduce_fusion = f32[128]{0:T(128)S(1)} fusion(bf16[128,2048]{1,0:T(8,128)(2,1)} %param.2), kind=kLoop, calls=%fused_computation.13 | loop fusion | flops 786304 | bytes 524800 | tf_op jit(solution)/shard_map/reduce_sum | solution.py:200
  7.3 6.6 %psum.7 = f32[128]{0:T(128)S(1)} all-reduce(f32[128]{0:T(128)S(1)} %multiply_reduce_fusion), channel_id=1, replica_groups=mesh['chan'=8,'seg'=4] {'seg'}, use_global_device_ids=true, to_apply=%region_1.0 | all-reduce | flops 128 | bytes 1024 | tf_op jit(solution)/shard_map/psum | solution.py:200
  13.9 0.2 collective-permute-start.3
  14.1 0.0 collective-permute-start.2
  14.2 0.9 %fusion.7 = (s32[1,128,128]{2,1,0:T(8,128)S(1)}, s32[1,128,128]{2,1,0:T(8,128)S(1)}) fusion(s32[2,128,128]{2,1,0:T(8,128)} %param.3), kind=kLoop, calls=%fused_computation.24 | loop fusion | bytes 262144 | tf_op jit(solution)/shard_map/slice | solution.py:207
  15.0 0.1 copy.11
  15.1 2.1 %collective-permute-start.4 = (s32[128,128]{0,1:T(8,128)S(1)}, s32[128,128]{0,1:T(8,128)S(1)}, u32[]{:S(2)}, u32[]{:S(2)}) collective-permute-start(s32[128,128]{0,1:T(8,128)S(1)} %bitcast.10), channel_id=1, source_target_pairs={{4,0},{8,4},{12,8},{16,12},{20,16},{24,20},{28,24},{0,28},{5,1},{9... | collective-permute-start | bytes 196616 | tf_op jit(solution)/shard_map/ppermute | solution.py:28
  17.2 1.1 %fusion.4 = (bf16[32,2048]{1,0:T(8,128)(2,1)S(1)}, bf16[32,2048]{1,0:T(8,128)(2,1)S(1)}, bf16[32,2048]{1,0:T(8,128)(2,1)S(1)}, bf16[32,2048]{1,0:T(8,128)(2,1)S(1)}) fusion(bf16[128,2048]{1,0:T(8,128)(2,1)} %param.2), kind=kLoop, calls=%fused_computation.21 | loop fusion | bytes 1048576 | tf_op jit(solution)/shard_map/slice | solution.py:199
  18.3 1.8 %collective-permute-start.7 = (bf16[32,2048]{1,0:T(8,128)(2,1)S(1)}, bf16[32,2048]{1,0:T(8,128)(2,1)S(1)}, u32[]{:S(2)}, u32[]{:S(2)}) collective-permute-start(bf16[32,2048]{1,0:T(8,128)(2,1)S(1)} %get-tuple-element.5), channel_id=1, source_target_pairs={{16,0},{20,4},{24,8},{28,12},{0,16},{4,20},{8,24},{12,28},{17,1},{... | collective-permute-start | bytes 393224 | tf_op jit(solution)/shard_map/ppermute | solution.py:28
  20.1 0.1 copy.10
  20.2 0.0 collective-permute-done.3
  20.2 1.3 %collective-permute-start.6 = (bf16[32,2048]{1,0:T(8,128)(2,1)S(1)}, bf16[32,2048]{1,0:T(8,128)(2,1)S(1)}, u32[]{:S(2)}, u32[]{:S(2)}) collective-permute-start(bf16[32,2048]{1,0:T(8,128)(2,1)S(1)} %get-tuple-element.8), channel_id=1, source_target_pairs={{16,0},{20,4},{24,8},{28,12},{0,16},{4,20},{8,24},{12,28},{17,1},{... | collective-permute-start | bytes 393224 | tf_op jit(solution)/shard_map/ppermute | solution.py:28
  21.5 0.0 collective-permute-done.2
  21.5 1.8 %collective-permute-start.5 = (bf16[32,2048]{1,0:T(8,128)(2,1)S(1)}, bf16[32,2048]{1,0:T(8,128)(2,1)S(1)}, u32[]{:S(2)}, u32[]{:S(2)}) collective-permute-start(bf16[32,2048]{1,0:T(8,128)(2,1)S(1)} %get-tuple-element.6), channel_id=1, source_target_pairs={{16,0},{20,4},{24,8},{28,12},{0,16},{4,20},{8,24},{12,28},{17,1},{... | collective-permute-start | bytes 393224 | tf_op jit(solution)/shard_map/ppermute | solution.py:28
  23.3 0.1 multiply_multiply_fusion
  23.4 0.0 collective-permute-done.4
  23.4 1.3 %collective-permute-start = (bf16[32,2048]{1,0:T(8,128)(2,1)S(1)}, bf16[32,2048]{1,0:T(8,128)(2,1)S(1)}, u32[]{:S(2)}, u32[]{:S(2)}) collective-permute-start(bf16[32,2048]{1,0:T(8,128)(2,1)S(1)} %get-tuple-element.7), channel_id=1, source_target_pairs={{16,0},{20,4},{24,8},{28,12},{0,16},{4,20},{8,24},{12,28},{17,1},{... | collective-permute-start | bytes 393224 | tf_op jit(solution)/shard_map/ppermute | solution.py:28
  24.7 0.0 collective-permute-done.1
  24.7 1.5 %fusion.3 = bf16[256,2112]{1,0:T(8,128)(2,1)S(1)} fusion(bf16[128,2048]{1,0:T(8,128)(2,1)S(1)} %collective-permute-done.1, bf16[128,2048]{1,0:T(8,128)(2,1)} %param.2), kind=kLoop, calls=%fused_computation.5 | loop fusion | flops 4866048 | bytes 2129920 | tf_op jit(solution)/shard_map/concatenate | solution.py:204
  26.2 0.4 slice_dynamic-update-slice_fusion.6
  26.6 0.4 slice_dynamic-update-slice_fusion.5
  27.0 0.4 slice_dynamic-update-slice_fusion.4
  27.5 0.0 copy-done
  27.6 0.4 slice_dynamic-update-slice_fusion.3
  28.0 0.4 slice_dynamic-update-slice_fusion.2
  28.4 0.4 slice_dynamic-update-slice_fusion.1
  28.8 0.4 slice_dynamic-update-slice_fusion.near_ref
  29.2 6.7 %collective-permute-done.7.far_ref = bf16[32,2048]{1,0:T(8,128)(2,1)S(1)} collective-permute-done((bf16[32,2048]{1,0:T(8,128)(2,1)S(1)}, bf16[32,2048]{1,0:T(8,128)(2,1)S(1)}, u32[]{:S(2)}, u32[]{:S(2)}) %collective-permute-start.7) | collective-permute-done | bytes 131104 | tf_op jit(solution)/shard_map/ppermute | solution.py:28
  35.9 4.6 %shard_map.28.prior_ref = f32[80,256]{1,0:T(8,128)S(1)} custom-call(bf16[32,2048]{1,0:T(8,128)(2,1)S(1)} %collective-permute-done.7.far_ref, bf16[2048,2048]{1,0:T(8,128)(2,1)S(1)} %slice_dynamic-update-slice_fusion.near_ref, f32[32,256]{1,0:T(8,128)S(1)} %get-tuple-element.13.scale_ref, s32[32,256]{1,0:T(8,128)S(1)} %get-tuple-element.9.bins_ref, ...), custom_call_target="tpu_custom_call" | custom-call | flops 2181038080 | bytes 8388608 | tf_op jit(solution)/shard_map/pallas_call | solution.py:97
  40.5 0.0 collective-permute-done.6.far_ref
  40.5 4.5 %shard_map.29.prior_ref = f32[80,256]{1,0:T(8,128)S(1)} custom-call(bf16[32,2048]{1,0:T(8,128)(2,1)S(1)} %collective-permute-done.6.far_ref, bf16[2048,2048]{1,0:T(8,128)(2,1)S(1)} %slice_dynamic-update-slice_fusion.near_ref, f32[32,256]{1,0:T(8,128)S(1)} %get-tuple-element.14.scale_ref, s32[32,256]{1,0:T(8,128)S(1)} %get-tuple-element.10.bins_ref, ...), custom_call_target="tpu_custom_call" | custom-call | flops 2181038080 | bytes 8388608 | tf_op jit(solution)/shard_map/pallas_call | solution.py:97
  45.0 0.0 collective-permute-done.5.far_ref
  45.0 4.5 %shard_map.30.prior_ref = f32[80,256]{1,0:T(8,128)S(1)} custom-call(bf16[32,2048]{1,0:T(8,128)(2,1)S(1)} %collective-permute-done.5.far_ref, bf16[2048,2048]{1,0:T(8,128)(2,1)S(1)} %slice_dynamic-update-slice_fusion.near_ref, f32[32,256]{1,0:T(8,128)S(1)} %get-tuple-element.15.scale_ref, s32[32,256]{1,0:T(8,128)S(1)} %get-tuple-element.11.bins_ref, ...), custom_call_target="tpu_custom_call" | custom-call | flops 2181038080 | bytes 8388608 | tf_op jit(solution)/shard_map/pallas_call | solution.py:97
  49.5 0.0 collective-permute-done.far_ref
  49.5 4.5 %shard_map.31 = f32[80,256]{1,0:T(8,128)S(1)} custom-call(bf16[32,2048]{1,0:T(8,128)(2,1)S(1)} %collective-permute-done.far_ref, bf16[2048,2048]{1,0:T(8,128)(2,1)S(1)} %slice_dynamic-update-slice_fusion.near_ref, f32[32,256]{1,0:T(8,128)S(1)} %get-tuple-element.16.scale_ref, s32[32,256]{1,0:T(8,128)S(1)} %get-tuple-element.12.bins_ref, ...), custom_call_target="tpu_custom_call" | custom-call | flops 2181038080 | bytes 8388608 | tf_op jit(solution)/shard_map/pallas_call | solution.py:97
  54.0 0.1 copy.8
  54.1 9.3 %shard_map.32 = f32[32,128]{1,0:T(8,128)S(1)} custom-call(f32[256,128]{1,0:T(8,128)S(1)} %pad.9.part_ref), custom_call_target="tpu_custom_call" | custom-call | tf_op jit(solution)/shard_map/pallas_call | solution.py:169
  63.4 0.7 %rev.3 = f32[65,32]{0,1:T(8,128)} reverse(f32[65,32]{0,1:T(8,128)S(1)} %bitcast.8), dimensions={0} | reverse | bytes 16640 | tf_op jit(solution)/shard_map/rev | solution.py:215
  (10 shorter events, 0.1 us)
Async XLA Ops:
  0.0 27.5 %copy-start = (bf16[128,2048]{1,0:T(8,128)(2,1)S(1)}, bf16[128,2048]{1,0:T(8,128)(2,1)}, u32[]{:S(2)}) copy-start(bf16[128,2048]{1,0:T(8,128)(2,1)} %param.2) | copy-start | bytes 1572868
  0.0 24.7 %collective-permute-start.1 = (bf16[128,2048]{1,0:T(8,128)(2,1)}, bf16[128,2048]{1,0:T(8,128)(2,1)S(1)}, u32[]{:S(2)}, u32[]{:S(2)}) collective-permute-start(bf16[128,2048]{1,0:T(8,128)(2,1)} %param.2), channel_id=1, source_target_pairs={{4,0},{8,4},{12,8},{16,12},{20,16},{24,20},{28,24},{0,28},{5,1},{9... | collective-permute-start | bytes 1572872 | tf_op jit(solution)/shard_map/ppermute | solution.py:28
  13.9 6.3 %collective-permute-start.3 = (f32[128]{0:T(128)S(1)}, f32[128]{0:T(128)S(1)}, u32[]{:S(2)}, u32[]{:S(2)}) collective-permute-start(f32[128]{0:T(128)S(1)} %add_rsqrt_fusion), channel_id=1, source_target_pairs={{4,0},{8,4},{12,8},{16,12},{20,16},{24,20},{28,24},{0,28},{5,1},{9... | collective-permute-start | bytes 1544 | tf_op jit(solution)/shard_map/ppermute | solution.py:28
  14.1 7.4 %collective-permute-start.2 = (f32[128]{0:T(128)S(1)}, f32[128]{0:T(128)S(1)}, u32[]{:S(2)}, u32[]{:S(2)}) collective-permute-start(f32[128]{0:T(128)S(1)} %add_rsqrt_fusion), channel_id=1, source_target_pairs={{16,0},{20,4},{24,8},{28,12},{0,16},{4,20},{8,24},{12,28},{17,1},{... | collective-permute-start | bytes 1544 | tf_op jit(solution)/shard_map/ppermute | solution.py:28
  15.1 8.3 %collective-permute-start.4 = (s32[128,128]{0,1:T(8,128)S(1)}, s32[128,128]{0,1:T(8,128)S(1)}, u32[]{:S(2)}, u32[]{:S(2)}) collective-permute-start(s32[128,128]{0,1:T(8,128)S(1)} %bitcast.10), channel_id=1, source_target_pairs={{4,0},{8,4},{12,8},{16,12},{20,16},{24,20},{28,24},{0,28},{5,1},{9... | collective-permute-start | bytes 196616 | tf_op jit(solution)/shard_map/ppermute | solution.py:28
  18.3 17.5 %collective-permute-start.7 = (bf16[32,2048]{1,0:T(8,128)(2,1)S(1)}, bf16[32,2048]{1,0:T(8,128)(2,1)S(1)}, u32[]{:S(2)}, u32[]{:S(2)}) collective-permute-start(bf16[32,2048]{1,0:T(8,128)(2,1)S(1)} %get-tuple-element.5), channel_id=1, source_target_pairs={{16,0},{20,4},{24,8},{28,12},{0,16},{4,20},{8,24},{12,28},{17,1},{... | collective-permute-start | bytes 393224 | tf_op jit(solution)/shard_map/ppermute | solution.py:28
  20.2 20.3 %collective-permute-start.6 = (bf16[32,2048]{1,0:T(8,128)(2,1)S(1)}, bf16[32,2048]{1,0:T(8,128)(2,1)S(1)}, u32[]{:S(2)}, u32[]{:S(2)}) collective-permute-start(bf16[32,2048]{1,0:T(8,128)(2,1)S(1)} %get-tuple-element.8), channel_id=1, source_target_pairs={{16,0},{20,4},{24,8},{28,12},{0,16},{4,20},{8,24},{12,28},{17,1},{... | collective-permute-start | bytes 393224 | tf_op jit(solution)/shard_map/ppermute | solution.py:28
  21.5 23.5 %collective-permute-start.5 = (bf16[32,2048]{1,0:T(8,128)(2,1)S(1)}, bf16[32,2048]{1,0:T(8,128)(2,1)S(1)}, u32[]{:S(2)}, u32[]{:S(2)}) collective-permute-start(bf16[32,2048]{1,0:T(8,128)(2,1)S(1)} %get-tuple-element.6), channel_id=1, source_target_pairs={{16,0},{20,4},{24,8},{28,12},{0,16},{4,20},{8,24},{12,28},{17,1},{... | collective-permute-start | bytes 393224 | tf_op jit(solution)/shard_map/ppermute | solution.py:28
  23.4 26.1 %collective-permute-start = (bf16[32,2048]{1,0:T(8,128)(2,1)S(1)}, bf16[32,2048]{1,0:T(8,128)(2,1)S(1)}, u32[]{:S(2)}, u32[]{:S(2)}) collective-permute-start(bf16[32,2048]{1,0:T(8,128)(2,1)S(1)} %get-tuple-element.7), channel_id=1, source_target_pairs={{16,0},{20,4},{24,8},{28,12},{0,16},{4,20},{8,24},{12,28},{17,1},{... | collective-permute-start | bytes 393224 | tf_op jit(solution)/shard_map/ppermute | solution.py:28

commit v3 on v0

v3 whole, which is shorter than its diff:
```python
import functools
import math

import jax
import jax.numpy as jnp
from jax import lax
from jax.experimental import pallas as pl
from jax.experimental.pallas import tpu as pltpu
from jax.sharding import PartitionSpec as P

MAX_LAG = 32
NB = 256
ROUNDS = 2
LAGS = 2 * MAX_LAG + 1
EPSILON = 1e-06

FINE = 8
COARSE = MAX_LAG // FINE
LANES = 128
CHUNKS = 4
MESH = pl.DeviceIdType.MESH
CONTRACT = (((1,), (1,)), ((), ()))


def whole_kernel(
    n_chan, n_seg, group, total_time, factor,
    traces_ref, energy_ref, bins_ref, later_bins_ref, out_ref,
    near, next_block, next_bins, far, scale_rows, energies, mine, scales_in,
    fine, neg, pos, last, total, part, arrived, second, others,
    send_e, recv_e, send_s, recv_s, send_n, recv_n, send_f, recv_f, send_1, recv_1, send_2, recv_2,
):
    chan, seg = lax.axis_index("chan"), lax.axis_index("seg")
    channels, length = traces_ref.shape
    width = 2 * channels
    size = channels // CHUNKS
    half = n_chan // 2
    rows = out_ref.shape[0]
    chan_peers = [lax.rem(chan + k, n_chan) for k in range(1, n_chan)]
    seg_peers = [lax.rem(seg + k, n_seg) for k in range(1, n_seg)]
    one_back = lax.rem(chan + n_chan - 1, n_chan)
    half_back = lax.rem(chan + n_chan - half, n_chan)

    def remote(source, target, send, recv, chan_to, seg_to):
        return pltpu.make_async_remote_copy(
            src_ref=source,
            dst_ref=target,
            send_sem=send,
            recv_sem=recv,
            device_id=(chan_to, seg_to),
            device_id_type=MESH,
        )

    def segment_sum(own, received):
        for position in range(n_seg):
            slot = lax.rem(seg - position + 2 * n_seg - 1, n_seg)
            term = jnp.where(slot == n_seg - 1, own, received[jnp.minimum(slot, n_seg - 2)])
            sums = term if position == 0 else sums + term
        return sums

    def dot(left, right):
        return lax.dot_general(left, right, CONTRACT, preferred_element_type=jnp.float32)

    barrier = pltpu.get_barrier_semaphore()
    for peer in chan_peers:
        pl.semaphore_signal(barrier, inc=1, device_id=(peer, seg), device_id_type=MESH)
    for peer in seg_peers:
        pl.semaphore_signal(barrier, inc=1, device_id=(chan, peer), device_id_type=MESH)
    pl.semaphore_wait(barrier, n_chan + n_seg - 2)

    energy_copies = [
        remote(energy_ref, energies.at[k], send_e.at[k], recv_e.at[k], chan, peer) for k, peer in enumerate(seg_peers)
    ]
    next_copies = [
        remote(traces_ref, next_block, send_n.at[0], recv_n.at[0], one_back, seg),
        remote(later_bins_ref, next_bins, send_n.at[1], recv_n.at[1], one_back, seg),
    ]
    for copy in energy_copies + next_copies:
        copy.start()
    for copy in energy_copies:
        copy.wait()
    own_scale = lax.rsqrt(segment_sum(energy_ref[...], energies) / total_time + EPSILON)
    mine[...] = own_scale
    scale_copies = [
        remote(mine, scales_in.at[k], send_s.at[k], recv_s.at[k], peer, seg)
        for k, peer in enumerate((one_back, half_back))
    ]
    for copy in scale_copies:
        copy.start()

    def far_copy(k):
        start = pl.multiple_of(k * size, size)
        return remote(traces_ref.at[pl.ds(start, size)], far.at[k], send_f.at[k], recv_f.at[k], half_back, seg)

    for k in range(CHUNKS):
        far_copy(k).start()

    tile = 16
    margin = jnp.zeros((tile, LANES), jnp.float32)

    def spread(source, offset):
        @pl.loop(0, channels // tile)
        def _(g):
            start = pl.multiple_of(g * tile, tile)
            block = source[pl.ds(start, tile), :]
            wide = jnp.concatenate([block.astype(jnp.float32), margin], 1)
            for k in range(2 * COARSE):
                shift = (k - COARSE + 1) * FINE
                if shift:
                    moved = pltpu.roll(wide, -shift % (length + LANES), 1)[:, :length].astype(jnp.bfloat16)
                else:
                    moved = block
                near[pl.ds(pl.multiple_of(k * width + offset + start, tile), tile), :] = moved

    spread(traces_ref, 0)
    for copy in next_copies:
        copy.wait()
    spread(next_block, channels)
    for copy in scale_copies:
        copy.wait()
    far_scale = jnp.transpose(jnp.broadcast_to(scales_in[1][:1], (channels, channels))) * (1.0 / math.sqrt(total_time))
    scale_rows[:, :channels] = far_scale * jnp.broadcast_to(mine[:1], (channels, channels))
    scale_rows[:, channels:] = far_scale * jnp.broadcast_to(scales_in[0][:1], (channels, channels))

    bin_ids = lax.broadcasted_iota(jnp.int32, (NB, width), 0)
    total[...] = jnp.zeros_like(total)
    pair = 2
    blank = jnp.zeros((FINE, LANES), jnp.float32)

    @pl.loop(0, CHUNKS)
    def _(chunk):
        far_copy(chunk).wait_recv()

        @pl.loop(0, size // tile)
        def _(g):
            wide = far[chunk, pl.ds(pl.multiple_of(g * tile, tile), tile), :].astype(jnp.float32)
            for start in range(0, tile, pair):
                both = []
                for x in range(start, start + pair):
                    row = jnp.broadcast_to(wide[x : x + 1], (FINE, length))
                    both.append(jnp.concatenate([row, blank], 1))
                first = pl.multiple_of((g * tile + start) * FINE, pair * FINE)
                for side, base in ((0, LANES + length - FINE), (1, 0)):
                    turned = [pltpu.roll(row, base, 1, stride=1, stride_axis=0)[:, :length] for row in both]
                    fine[side, pl.ds(first, pair * FINE), :] = jnp.concatenate(turned, 0).astype(jnp.bfloat16)

        neg[...] = dot(fine[0], near[: COARSE * width])
        pos[...] = dot(fine[1], near[(COARSE - 1) * width : (2 * COARSE - 1) * width])
        last[...] = dot(far[chunk], near[(2 * COARSE - 1) * width :])

        @pl.loop(0, size // group)
        def _(g):
            base = pl.multiple_of(g * group, group)
            here = pl.ds(pl.multiple_of(chunk * size + base, group), group)
            scale = scale_rows[here, :]
            bins = jnp.concatenate([bins_ref[here, :], next_bins[here, :]], 1)
            top = last[pl.ds(base, group), :]
            for first in range(0, group, group // 2):
                scores, hots = [], []
                for x in range(first, first + group // 2):
                    lines = pl.ds(pl.multiple_of((base + x) * FINE, FINE), FINE)
                    weight = jnp.broadcast_to(scale[x : x + 1], (FINE, width))
                    pieces = []
                    for side in (neg, pos):
                        for k in range(COARSE):
                            pieces.append(side[lines, k * width : (k + 1) * width] * weight)
                    edge = jnp.broadcast_to(top[x : x + 1], (FINE, width)) * weight
                    pieces += [edge, edge]
                    scores.append(jnp.concatenate(pieces, 0).astype(jnp.bfloat16))
                    hit = jnp.broadcast_to(bins[x : x + 1], (NB, width)) == bin_ids
                    hots.append(jnp.where(hit, 1.0, 0.0).astype(jnp.bfloat16))
                total[...] += dot(jnp.concatenate(scores, 1), jnp.concatenate(hots, 1))

    filler = jnp.zeros((LANES - total.shape[0], NB), jnp.float32)
    part[...] = jnp.transpose(jnp.concatenate([total[...] * factor, filler], 0))

    first_copies = []
    for k, peer in enumerate(chan_peers):
        owned = pl.ds(pl.multiple_of(peer * rows, rows), rows)
        first_copies.append(remote(part.at[owned], arrived.at[k], send_1.at[k], recv_1.at[k], peer, seg))
    for copy in first_copies:
        copy.start()
    running = part[pl.ds(pl.multiple_of(chan * rows, rows), rows), :]
    for k, copy in enumerate(first_copies):
        copy.wait()
        running = running + arrived[k]
    second[...] = running
    second_copies = [
        remote(second, others.at[k], send_2.at[k], recv_2.at[k], chan, peer) for k, peer in enumerate(seg_peers)
    ]
    for copy in second_copies:
        copy.start()
    for copy in second_copies:
        copy.wait()
    out_ref[...] = segment_sum(second[...], others)
    for k in range(CHUNKS):
        far_copy(k).wait_send()


def local(traces, pair_bins):
    channels, length = traces.shape
    n_chan, n_seg = lax.axis_size("chan"), lax.axis_size("seg")
    total_time = length * n_seg
    pair_total = ROUNDS * n_chan * channels * channels // NB
    energy = jnp.sum(jnp.square(traces.astype(jnp.float32)), axis=1)
    energy = jnp.broadcast_to(energy[None], (8, channels))
    width, size, rows = 2 * channels, channels // CHUNKS, NB // n_chan
    lag_rows = 2 * MAX_LAG + 2 * FINE
    f32, bf16 = jnp.float32, jnp.bfloat16
    counts = (n_seg - 1, 2, 2, CHUNKS, n_chan - 1, n_seg - 1)
    out = pl.pallas_call(
        functools.partial(whole_kernel, n_chan, n_seg, 8, total_time, 1.0 / math.sqrt(pair_total)),
        out_shape=jax.ShapeDtypeStruct((rows, LANES), f32),
        in_specs=[pl.BlockSpec(memory_space=pltpu.VMEM)] * 4,
        out_specs=pl.BlockSpec(memory_space=pltpu.VMEM),
        scratch_shapes=[
            pltpu.VMEM((2 * COARSE * width, length), bf16),
            pltpu.VMEM((channels, length), bf16),
            pltpu.VMEM((channels, channels), jnp.int32),
            pltpu.VMEM((CHUNKS, size, length), bf16),
            pltpu.VMEM((channels, width), f32),
            pltpu.VMEM((n_seg - 1, 8, channels), f32),
            pltpu.VMEM((8, channels), f32),
            pltpu.VMEM((2, 8, channels), f32),
            pltpu.VMEM((2, size * FINE, length), bf16),
            pltpu.VMEM((size * FINE, COARSE * width), f32),
            pltpu.VMEM((size * FINE, COARSE * width), f32),
            pltpu.VMEM((size, width), f32),
            pltpu.VMEM((lag_rows, NB), f32),
            pltpu.VMEM((NB, LANES), f32),
            pltpu.VMEM((n_chan - 1, rows, LANES), f32),
            pltpu.VMEM((rows, LANES), f32),
            pltpu.VMEM((n_seg - 1, rows, LANES), f32),
        ]
        + [pltpu.SemaphoreType.DMA((count,)) for count in counts for _ in range(2)],
        compiler_params=pltpu.CompilerParams(
            collective_id=0, has_side_effects=True, vmem_limit_bytes=40 * 1024 * 1024
        ),
    )(traces, energy, pair_bins[0].T, pair_bins[1].T)
    return out.T[:LAGS][::-1]


def solution(mesh):
    in_specs = (P("chan", "seg"), P(None, "chan", None))
    out_specs = P(None, "chan")
    return jax.shard_map(local, mesh=mesh, in_specs=in_specs, out_specs=out_specs, check_vma=False)
```

time: 283 us -> 65.4 us (0.23)
  waiting for transfers between devices: 106 us -> 0 us
  matrix products: 66.7 us -> 0 us
  Pallas kernels: 0 us -> 63.2 us
  local copies, waits for them, and re-layouts: 51.9 us -> 1.81 us
  loops' own time: 18.2 us -> 0 us
  blocking collectives: 16.1 us -> 0 us
  between operations: 13.6 us -> 0.04 us
  starting transfers between devices: 5.36 us -> 0 us
  other arithmetic: 4.33 us -> 0.19 us
    unnamed x2 -> x0, waiting for transfers between devices: 73.5 us -> none
    dot_general x146 -> x0, matrix products: 66.7 us -> none  [the longest x130 49.9 us: lag_block(): lax.dot_general(own_block, shifted, (((1,), (1,)), ((), ())), preferred_e...]
    pallas_call x0 -> x1, Pallas kernels: none -> 63.2 us  [local(): pl.pallas_call(functools.partial(whole_kernel, n_chan, n_seg, 8, total_ti...]
    ppermute x2 -> x0, waiting for transfers between devices: 32.1 us -> none  [from_behind(): return lax.ppermute(block, axis, route)]
    another operation x4 -> x0, loops' own time: 18.2 us -> none  [the longest x2 11.2 us: round_stack(): lax.scan(bin_step, running, jnp.arange(channels // row_block, dtype=jnp.i...]
    dynamic_slice x42 -> x0, local copies, waits for them, and re-layouts: 16.6 us -> none  [the longest x16 10.4 us: round_stack(): lax.scan(bin_step, running, jnp.arange(channels // row_block, dtype=jnp.i...]
    psum x2 -> x0, blocking collectives: 16.1 us -> none  [the longest x1 10.5 us: local(): summed = lax.psum(partial_value, 'seg')]
    unnamed x16 -> x4, local copies, waits for them, and re-layouts: 15.2 us -> 0.18 us
  transfers between devices with their start and end apart: 3 -> 0, of which waited for: 2 -> 0; matrix products, arithmetic and copies ran while one was open for 1% -> 0% of each run, Pallas kernels for 0% -> 0%
where the time goes in v3:
time: 65.4 us; the launch traced here: 65.2 us
  Pallas kernels  63.2 us (97%)
  local copies, waits for them, and re-layouts  1.81 us (3%)
    pallas_call x1, Pallas kernels, local(): pl.pallas_call(functools.partial(whole_kernel, n_chan, n_seg, 8, total_ti...  63.2 us

profile of v3, /device:TPU:0, one launch (start us, length us, event | category | flops | bytes accessed | tf_op | source)
XLA Modules:
  0.0 65.2 jit_solution(9645652978590257381)
XLA Ops:
  0.0 0.0 copy-start
  0.0 0.9 %fusion = (s32[1,128,128]{2,1,0:T(8,128)S(1)}, s32[1,128,128]{2,1,0:T(8,128)S(1)}) fusion(s32[2,128,128]{2,1,0:T(8,128)} %param.3), kind=kLoop, calls=%fused_computation.1 | loop fusion | bytes 262144 | tf_op jit(solution)/shard_map/slice | solution.py:238
  0.9 0.1 copy.5
  1.0 0.1 copy.6
  1.1 0.0 copy-done
  1.2 0.2 multiply_reduce_fusion
  1.3 63.2 %shard_map.28 = f32[32,128]{1,0:T(8,128)S(1)} custom-call(bf16[128,2048]{1,0:T(8,128)(2,1)S(1)} %copy-done, f32[8,128]{1,0:T(8,128)S(1)} %broadcast_in_dim.2.energy_ref, s32[128,128]{1,0:T(8,128)S(1)} %bitcast.8, s32[128,128]{1,0:T(8,128)S(1)} %bitcast.9), custom_call_target="tpu_custom_call" | custom-call | tf_op jit(solution)/shard_map/pallas_call | solution.py:210
  64.5 0.7 %rev.3 = f32[65,32]{0,1:T(8,128)} reverse(f32[65,32]{0,1:T(8,128)S(1)} %bitcast.10), dimensions={0} | reverse | bytes 16640 | tf_op jit(solution)/shard_map/rev | solution.py:239
  (1 shorter events, 0.0 us)
Async XLA Ops:
  0.0 1.1 %copy-start = (bf16[128,2048]{1,0:T(8,128)(2,1)S(1)}, bf16[128,2048]{1,0:T(8,128)(2,1)}, u32[]{:S(2)}) copy-start(bf16[128,2048]{1,0:T(8,128)(2,1)} %traces_ref.1) | copy-start | bytes 1572868

commit v4 on v3

--- a/solution.py
+++ b/solution.py
@@ -71,10 +71,10 @@
         remote(energy_ref, energies.at[k], send_e.at[k], recv_e.at[k], chan, peer) for k, peer in enumerate(seg_peers)
     ]
     next_copies = [
+        remote(later_bins_ref, next_bins, send_n.at[1], recv_n.at[1], one_back, seg),
         remote(traces_ref, next_block, send_n.at[0], recv_n.at[0], one_back, seg),
-        remote(later_bins_ref, next_bins, send_n.at[1], recv_n.at[1], one_back, seg),
-    ]
-    for copy in energy_copies + next_copies:
+    ]
+    for copy in energy_copies:
         copy.start()
     for copy in energy_copies:
         copy.wait()
@@ -84,7 +84,7 @@
         remote(mine, scales_in.at[k], send_s.at[k], recv_s.at[k], peer, seg)
         for k, peer in enumerate((one_back, half_back))
     ]
-    for copy in scale_copies:
+    for copy in scale_copies + next_copies:
         copy.start()
 
     def far_copy(k):

time: 65.4 us -> 67.5 us (1.032)
  Pallas kernels: 63.2 us -> 65.4 us
    pallas_call x1, Pallas kernels: 63.2 us -> 65.4 us  [local(): pl.pallas_call(functools.partial(whole_kernel, n_chan, n_seg, 8, total_ti...]
where the time goes in v4:
time: 67.5 us; the launch traced here: 67.4 us
  Pallas kernels  65.4 us (97%)
  local copies, waits for them, and re-layouts  1.81 us (3%)
    pallas_call x1, Pallas kernels, local(): pl.pallas_call(functools.partial(whole_kernel, n_chan, n_seg, 8, total_ti...  65.4 us

profile of v4, /device:TPU:0, one launch (start us, length us, event | category | flops | bytes accessed | tf_op | source)
XLA Modules:
  0.0 67.4 jit_solution(10231429112205716336)
XLA Ops:
  0.0 0.0 copy-start
  0.0 0.9 %fusion = (s32[1,128,128]{2,1,0:T(8,128)S(1)}, s32[1,128,128]{2,1,0:T(8,128)S(1)}) fusion(s32[2,128,128]{2,1,0:T(8,128)} %param.3), kind=kLoop, calls=%fused_computation.1 | loop fusion | bytes 262144 | tf_op jit(solution)/shard_map/slice | solution.py:238
  0.9 0.1 copy.5
  1.0 0.1 copy.6
  1.1 0.0 copy-done
  1.2 0.2 multiply_reduce_fusion
  1.3 65.4 %shard_map.28 = f32[32,128]{1,0:T(8,128)S(1)} custom-call(bf16[128,2048]{1,0:T(8,128)(2,1)S(1)} %copy-done, f32[8,128]{1,0:T(8,128)S(1)} %broadcast_in_dim.2.energy_ref, s32[128,128]{1,0:T(8,128)S(1)} %bitcast.8, s32[128,128]{1,0:T(8,128)S(1)} %bitcast.9), custom_call_target="tpu_custom_call" | custom-call | tf_op jit(solution)/shard_map/pallas_call | solution.py:210
  66.7 0.7 %rev.3 = f32[65,32]{0,1:T(8,128)} reverse(f32[65,32]{0,1:T(8,128)S(1)} %bitcast.10), dimensions={0} | reverse | bytes 16640 | tf_op jit(solution)/shard_map/rev | solution.py:239
  (1 shorter events, 0.0 us)
Async XLA Ops:
  0.0 1.1 %copy-start = (bf16[128,2048]{1,0:T(8,128)(2,1)S(1)}, bf16[128,2048]{1,0:T(8,128)(2,1)}, u32[]{:S(2)}) copy-start(bf16[128,2048]{1,0:T(8,128)(2,1)} %traces_ref.1) | copy-start | bytes 1572868
